TPU v7x, 256 devices: a whole 4x4x8 slice. The times are simulated.
256 devices in a mesh: tm: 32 (over x, z_hi, core), head: 8 (over z_lo, y).
Axes of the slice: x: 4, y: 4, z: 8 (z_hi: 4, z_lo: 2; z = z_hi * 2 + z_lo), core: 2. Of those that a mesh axis runs over, the one named last changes fastest.
Arguments:
- query_states: bfloat16 [49152, 1024], P('tm', 'head'), may hold values from -30 to 30
- key_states: bfloat16 [49152, 1024], P('tm', 'head'), may hold values from -30 to 30
- value_states: bfloat16 [49152, 1024], P('tm', 'head'), may hold values from -6 to 6
- win_start: int32 [64], P('tm'), may hold values from 0 to 62, as said below
- group_end: int32 [64], P('tm'), may hold values from 0 to 63, as said below
- out_weight: bfloat16 [1024, 1536], replicated, may hold values from -0.1875 to 0.1875
Outputs:
- projected: bfloat16 [49152, 1536], P(('tm', 'head'))
Inputs may be any that keep to these rules, and one draw needn't show every extreme that they name: For every frame f, win_start[f] = max(f - lag, 0) with a lag of 1 to 3; frame 64 - 2 has a lag of 3 in every draw, and the last frame has a lag of 1. `group_end`: frames 2p and 2p + 1 form one group (both end at 2p + 1) or two groups of one frame (each ends at itself); both kinds occur in every draw.
All inputs are finite; a program needn't handle non-finite values.
Results may differ from a plain program's by a relative error of at most 0.0051.
Values may be sent and summed in bfloat16 or wider, within the bound.
A program may use at most 64 MiB of HBM per device.

v0:
```python
import jax
import jax.numpy as jnp
from jax import lax
from jax.sharding import PartitionSpec as P

HD = 128
FT = 768


def spread(block, axis, owner):
    block = jnp.where(lax.axis_index(axis) == owner, block, jnp.zeros_like(block))
    return lax.psum(block, axis)


def from_behind(array, axis, by):
    length = lax.axis_size(axis)
    pairs = [(i, i + by) for i in range(length) if 0 <= i + by < length]
    return lax.ppermute(array, axis, pairs)


def attend(query_rows, key_rows, value_rows, visible):
    heads_here = query_rows.shape[1] // HD
    query_heads = query_rows.reshape(query_rows.shape[0], heads_here, HD)
    key_heads = key_rows.reshape(key_rows.shape[0], heads_here, HD)
    value_heads = value_rows.reshape(value_rows.shape[0], heads_here, HD)
    scores = jnp.einsum(
        "qhd,khd->hqk", query_heads, key_heads, preferred_element_type=jnp.float32
    ) * HD ** (-0.5)
    scores = jnp.where(visible[None, None, :], scores, -1e30)
    peak = jnp.max(scores, axis=-1, keepdims=True)
    weights = jnp.where(visible[None, None, :], jnp.exp(scores - peak), 0.0)
    total = jnp.sum(weights, axis=-1)
    rounded = weights.astype(jnp.bfloat16)
    mixed = jnp.einsum("hqk,khd->qhd", rounded, value_heads, preferred_element_type=jnp.float32)
    mixed = mixed / jnp.transpose(total)[:, :, None]
    return mixed.astype(jnp.bfloat16).reshape(query_rows.shape[0], query_rows.shape[1])


def local(query_states, key_states, value_states, win_start, group_end, out_weight):
    local_frames = win_start.shape[0]
    stacked = jnp.stack([key_states, value_states])
    sink_frame = stacked[:, :FT]
    sink_states = spread(sink_frame, "tm", 0)
    near_count = min(3, local_frames)
    far_count = 3 - near_count
    near_frames = from_behind(stacked, "tm", 1)
    pieces = []
    far_frames = from_behind(stacked[:, (local_frames - far_count) * FT :], "tm", 2)
    pieces.append(far_frames)
    extended = jnp.concatenate(pieces + [near_frames, stacked], axis=1)
    first_id = lax.axis_index("tm") * local_frames - 3
    outputs = []
    for slot in range(local_frames):
        span_frames = 5 if slot % 2 == 0 else 4
        window = extended[:, slot * FT : (slot + span_frames) * FT]
        key_rows = jnp.concatenate([sink_states[0], window[0]], axis=0)
        value_rows = jnp.concatenate([sink_states[1], window[1]], axis=0)
        frame_ids = first_id + slot + jnp.arange(span_frames * FT, dtype=jnp.int32) // FT
        window_seen = (
            (frame_ids >= 1) & (frame_ids >= win_start[slot]) & (frame_ids <= group_end[slot])
        )
        visible = jnp.concatenate([jnp.ones((FT,), dtype=bool), window_seen])
        query_rows = query_states[slot * FT : (slot + 1) * FT]
        outputs.append(attend(query_rows, key_rows, value_rows, visible))
    attended = jnp.concatenate(outputs, axis=0)
    token_rows = lax.all_to_all(attended, "head", split_axis=0, concat_axis=1, tiled=True)
    return jnp.dot(token_rows, out_weight, preferred_element_type=jnp.float32).astype(jnp.bfloat16)


def solution(mesh):
    in_specs = (P("tm", "head"), P("tm", "head"), P("tm", "head"), P("tm"), P("tm"), P())
    out_specs = P(("tm", "head"), None)
    return jax.shard_map(local, mesh=mesh, in_specs=in_specs, out_specs=out_specs, check_vma=False)
```

profile of v0, /device:TPU:8, one launch (start us, length us, event | category | flops | bytes accessed | tf_op | source)
XLA Modules:
  0.0 344.9 jit_solution(8197452554077602024)
XLA Ops:
  6.5 0.0 copy-start
  6.5 0.0 all-reduce.4.cloned.1.call-start
  6.5 2.2 pad_maximum_fusion
  8.8 2.6 collective-permute-start.1
  11.4 2.2 fusion.58
  13.6 0.0 all-reduce.4.cloned.1.call-update
  13.6 5.2 %collective-permute-start = (bf16[2,768,128]{2,1,0:T(8,128)(2,1)}, bf16[2,768,128]{2,1,0:T(8,128)(2,1)}, u32[]{:S(2)}, u32[]{:S(2)}) collective-permute-start(bf16[2,768,128]{2,1,0:T(8,128)(2,1)} %get-tuple-element.9), channel_id=1, source_target_pairs={{0,16},{8,24},{16,32},{24,40},{32,48},{40,56},{48,64},{56,72},{64,... | collective-permute-start | bytes 1179656 | tf_op jit(solution)/shard_map/ppermute | solution.py:18
  18.8 1.3 fusion.81
  20.2 1.3 fusion.82
  21.4 1.1 compare_and_fusion.1
  22.6 1.2 compare_and_fusion
  23.8 275.4 %all-reduce.4.cloned.1.call-done = bf16[2,768,128]{2,1,0:T(8,128)(2,1)} async-done(((bf16[2,768,128]{2,1,0:T(8,128)(2,1)}), bf16[2,768,128]{2,1,0:T(8,128)(2,1)}) %all-reduce.4.cloned.1.call-update) | async-done | bytes 393232 | tf_op jit(solution)/shard_map/psum | solution.py:12
  299.2 1.1 slice_bitcast_fusion.5
  300.3 0.0 collective-permute-done.1
  300.3 1.5 maximum_maximum_fusion.1
  301.8 0.0 copy-start.3
  301.8 0.1 slice_bitcast_fusion.3
  301.9 0.0 collective-permute-done
  301.9 0.0 copy-done.1
  301.9 0.0 copy-done.2
  301.9 1.4 maximum_maximum_fusion
  303.3 0.1 slice_bitcast_fusion.1
  303.4 0.0 copy-done.3
  303.4 1.9 fusion.1
  305.4 3.9 %fusion.4 = f32[768]{0:T(1024)S(1)} fusion(f32[3840,768]{1,0:T(8,128)S(1)} %get-tuple-element.18, f32[768]{0:T(1024)S(1)} %get-tuple-element.17, pred[3840]{0:T(1024)(128)(4,1)S(1)} %concatenate.33), kind=kLoop, calls=%fused_computation.8 | loop fusion | flops 14744832 | bytes 11806464 | tf_op jit(solution)/shard_map/reduce_sum | solution.py:32
  309.3 2.3 fusion
  311.6 4.5 %fusion.2 = f32[768]{0:T(1024)S(1)} fusion(f32[4608,768]{1,0:T(8,128)S(1)} %get-tuple-element.20, f32[768]{0:T(1024)S(1)} %get-tuple-element.19, pred[4608]{0:T(1024)(128)(4,1)S(1)} %concatenate.29), kind=kLoop, calls=%fused_computation.6 | loop fusion | flops 17693952 | bytes 14166528 | tf_op jit(solution)/shard_map/reduce_sum | solution.py:32
  316.1 3.2 fusion.46
  319.4 3.8 %fusion.35 = bf16[768,128]{0,1:T(8,128)(2,1)S(1)} fusion(f32[4608,768]{1,0:T(8,128)S(1)} %get-tuple-element.20, f32[768]{0:T(1024)S(1)} %get-tuple-element.19, pred[4608]{0:T(1024)(128)(4,1)S(1)} %concatenate.29, bf16[3840,128]{1,0:T(8,128)(2,1)S(1)} %get-tuple-element.5, bf16[768,128]{1,0:T(8,128)(2,1)S(1)} %get-tuple-element.11, f32[768]{0:T(1024)S(1)} %fusion.2), kind=kOutput, calls=%fused_computation.28 | convolution fusion | flops 926220288 | bytes 15542784 | tf_op jit(solution)/shard_map/hqk,khd->qhd/dot_general | solution.py:34
  323.3 0.9 copy.7
  324.2 12.3 %all_to_all.19 = bf16[8,192,128]{2,1,0:T(8,128)(2,1)S(1)} all-to-all(bf16[8,192,128]{2,1,0:T(8,128)(2,1)} %bitcast.60), channel_id=1, replica_groups=mesh['tm'=32,'head'=8] {'head'}, dimensions={0} | all-to-all | bytes 786432 | tf_op jit(solution)/shard_map/all_to_all | solution.py:66
  336.5 1.6 convolution_convert_fusion
  (6 shorter events, 0.1 us)
Async XLA Ops:
  6.5 329.9 %copy-start = (bf16[1024,1536]{1,0:T(8,128)(2,1)S(1)}, bf16[1024,1536]{1,0:T(8,128)(2,1)}, u32[]{:S(2)}) copy-start(bf16[1024,1536]{1,0:T(8,128)(2,1)} %param.11) | copy-start | bytes 9437188
  6.5 295.4 %copy-start.1 = (bf16[1536,128]{1,0:T(8,128)(2,1)S(1)}, bf16[1536,128]{1,0:T(8,128)(2,1)}, u32[]{:S(2)}) copy-start(bf16[1536,128]{1,0:T(8,128)(2,1)} %param.8) | copy-start | bytes 1179652
  6.5 292.6 %all-reduce.4.cloned.1.call-start = ((), (), s32[]{:S(2)}) async-start(), calls=%async_computation.1 | async-start | bytes 786432 | tf_op jit(solution)/shard_map/psum | solution.py:12
  8.8 291.5 %collective-permute-start.1 = (bf16[2,1536,128]{2,1,0:T(8,128)(2,1)}, bf16[2,1536,128]{2,1,0:T(8,128)(2,1)}, u32[]{:S(2)}, u32[]{:S(2)}) collective-permute-start(bf16[2,1536,128]{2,1,0:T(8,128)(2,1)} %pad_maximum_fusion), channel_id=1, source_target_pairs={{0,8},{8,16},{16,24},{24,32},{32,40},{40,48},{48,56},{56,64},{64,7... | collective-permute-start | bytes 2359304 | tf_op jit(solution)/shard_map/ppermute | solution.py:18
  13.6 288.3 %collective-permute-start = (bf16[2,768,128]{2,1,0:T(8,128)(2,1)}, bf16[2,768,128]{2,1,0:T(8,128)(2,1)}, u32[]{:S(2)}, u32[]{:S(2)}) collective-permute-start(bf16[2,768,128]{2,1,0:T(8,128)(2,1)} %get-tuple-element.9), channel_id=1, source_target_pairs={{0,16},{8,24},{16,32},{24,40},{32,48},{40,56},{48,64},{56,72},{64,... | collective-permute-start | bytes 1179656 | tf_op jit(solution)/shard_map/ppermute | solution.py:18
  299.2 2.7 copy-start.2
  301.8 1.7 copy-start.3
Sparse Core Ops, SparseCore 0:
  13.7 285.4 all-reduce.3
where the time goes:
time: 345 us
  waiting for transfers between devices  275 us (80%)
  other arithmetic  18 us (5%)
  between operations  13.5 us (4%)
  matrix products  12.9 us (4%)
  blocking collectives  12.3 us (4%)
  starting transfers between devices  7.88 us (2%)
  local copies, waits for them, and re-layouts  4.87 us (1%)
    psum x1, waiting for transfers between devices, spread(): return lax.psum(block, axis)  275 us
    all_to_all x1, blocking collectives, local(): lax.all_to_all(attended, 'head', split_axis=0, concat_axis=1, tiled=True)  12.3 us
    reduce_sum x2, other arithmetic, attend(): total = jnp.sum(weights, axis=-1)  8.39 us
    ppermute x2, starting transfers between devices, from_behind(): return lax.ppermute(array, axis, pairs)  7.88 us
    dot_general x2, matrix products, attend(): jnp.einsum('hqk,khd->qhd', rounded, value_heads, preferred_element_type=j...  7.06 us
  transfers between devices with their start and end apart: 3, of which 1 were waited for; matrix products, arithmetic and copies ran while one was open for 3% of the time, Pallas kernels for 0%

commit v1 on v0

--- a/solution.py
+++ b/solution.py
@@ -9,7 +9,7 @@
 
 def spread(block, axis, owner):
     block = jnp.where(lax.axis_index(axis) == owner, block, jnp.zeros_like(block))
-    return lax.psum(block, axis)
+    return jnp.sum(lax.all_gather(block, axis), axis=0)
 
 
 def from_behind(array, axis, by):

time: 345 us -> 178 us (0.52)
  waiting for transfers between devices: 275 us -> 95.3 us
  other arithmetic: 18 us -> 25.2 us
    psum x1 -> x0, waiting for transfers between devices: 275 us -> none  [spread(): return lax.psum(block, axis)]
    all_gather x0 -> x1, waiting for transfers between devices: none -> 87.6 us  [spread(): return jnp.sum(lax.all_gather(block, axis), axis=0)]
    ppermute x2, waiting for transfers between devices: 0.01 us -> 7.75 us  [from_behind(): return lax.ppermute(array, axis, pairs)]
    reduce_sum x0 -> x1, other arithmetic: none -> 6.72 us  [spread(): return jnp.sum(lax.all_gather(block, axis), axis=0)]
  transfers between devices with their start and end apart: 3 -> 3, of which waited for: 1 -> 2; matrix products, arithmetic and copies ran while one was open for 3% -> 7% of each run, Pallas kernels for 0% -> 0%
where the time goes in v1:
time: 178 us; the launch traced here: 176 us
  waiting for transfers between devices  95.3 us (54%)
  other arithmetic  25.2 us (14%)
  matrix products  15.5 us (9%)
  between operations  13.6 us (8%)
  blocking collectives  12.5 us (7%)
  starting transfers between devices  7.86 us (4%)
  local copies, waits for them, and re-layouts  6.4 us (4%)
    all_gather x1, waiting for transfers between devices, spread(): return jnp.sum(lax.all_gather(block, axis), axis=0)  87.6 us
    all_to_all x1, blocking collectives, local(): lax.all_to_all(attended, 'head', split_axis=0, concat_axis=1, tiled=True)  12.5 us
    reduce_sum x2, other arithmetic, attend(): total = jnp.sum(weights, axis=-1)  8.4 us
    ppermute x2, starting transfers between devices, from_behind(): return lax.ppermute(array, axis, pairs)  7.85 us
    ppermute x2, waiting for transfers between devices, from_behind(): return lax.ppermute(array, axis, pairs)  7.75 us
    dot_general x2, matrix products, attend(): jnp.einsum('qhd,khd->hqk', query_heads, key_heads, preferred_element_type...  7.14 us
    dot_general x2, matrix products, attend(): jnp.einsum('hqk,khd->qhd', rounded, value_heads, preferred_element_type=j...  6.78 us
    reduce_sum x1, other arithmetic, spread(): return jnp.sum(lax.all_gather(block, axis), axis=0)  6.72 us
  transfers between devices with their start and end apart: 3, of which 2 were waited for; matrix products, arithmetic and copies ran while one was open for 7% of the time, Pallas kernels for 0%

profile of v1, /device:TPU:8, one launch (start us, length us, event | category | flops | bytes accessed | tf_op | source)
XLA Modules:
  0.0 176.4 jit_solution(18057666262837697530)
XLA Ops:
  6.5 0.0 copy-start
  6.5 0.0 all-gather.3.cloned.1.call-start
  6.5 2.3 %fusion.58 = (bf16[2,768,128]{2,1,0:T(8,128)(2,1)}, bf16[2,768,128]{2,1,0:T(8,128)(2,1)}) fusion(bf16[1,1536,128]{2,1,0:T(8,128)(2,1)} %bitcast.58, bf16[1,1536,128]{2,1,0:T(8,128)(2,1)} %bitcast.54, pred[]{:T(512)S(6)} %eq.3), kind=kLoop, calls=%fused_computation.50 | loop fusion | flops 589824 | bytes 1572865 | tf_op jit(solution)/shard_map/stack | solution.py:41
  8.9 0.0 all-gather.3.cloned.1.call-update
  8.9 2.1 %pad_maximum_fusion = bf16[2,1536,128]{2,1,0:T(8,128)(2,1)} fusion(bf16[1,1536,128]{2,1,0:T(8,128)(2,1)} %bitcast.55, bf16[1,1536,128]{2,1,0:T(8,128)(2,1)} %bitcast.59), kind=kLoop, calls=%fused_computation.34 | loop fusion | flops 393216 | bytes 1572864 | tf_op jit(solution)/shard_map/stack | solution.py:41
  11.0 2.6 %collective-permute-start.1 = (bf16[2,1536,128]{2,1,0:T(8,128)(2,1)}, bf16[2,1536,128]{2,1,0:T(8,128)(2,1)}, u32[]{:S(2)}, u32[]{:S(2)}) collective-permute-start(bf16[2,1536,128]{2,1,0:T(8,128)(2,1)} %pad_maximum_fusion), channel_id=1, source_target_pairs={{0,8},{8,16},{16,24},{24,32},{32,40},{40,48},{48,56},{56,64},{64,7... | collective-permute-start | bytes 2359304 | tf_op jit(solution)/shard_map/ppermute | solution.py:18
  13.6 5.2 %collective-permute-start = (bf16[2,768,128]{2,1,0:T(8,128)(2,1)}, bf16[2,768,128]{2,1,0:T(8,128)(2,1)}, u32[]{:S(2)}, u32[]{:S(2)}) collective-permute-start(bf16[2,768,128]{2,1,0:T(8,128)(2,1)} %get-tuple-element.9), channel_id=1, source_target_pairs={{0,16},{8,24},{16,32},{24,40},{32,48},{40,56},{48,64},{56,72},{64,... | collective-permute-start | bytes 1179656 | tf_op jit(solution)/shard_map/ppermute | solution.py:18
  18.9 1.4 fusion.81
  20.3 1.3 fusion.82
  21.6 1.3 compare_and_fusion
  22.9 1.3 compare_and_fusion.1
  24.2 0.0 collective-permute-done.1
  24.2 1.6 maximum_maximum_fusion.1
  25.7 7.7 %collective-permute-done = bf16[2,768,128]{2,1,0:T(8,128)(2,1)} collective-permute-done((bf16[2,768,128]{2,1,0:T(8,128)(2,1)}, bf16[2,768,128]{2,1,0:T(8,128)(2,1)}, u32[]{:S(2)}, u32[]{:S(2)}) %collective-permute-start) | collective-permute-done | bytes 393248 | tf_op jit(solution)/shard_map/ppermute | solution.py:18
  33.5 0.0 copy-done.1
  33.5 1.5 maximum_maximum_fusion
  35.0 1.3 slice_bitcast_fusion.3
  36.3 1.4 slice_bitcast_fusion.1
  37.7 87.6 %all-gather.3.cloned.1.call-done = bf16[64,768,128]{2,1,0:T(8,128)(2,1)} async-done(((bf16[2,768,128]{2,1,0:T(8,128)(2,1)}), bf16[64,768,128]{2,1,0:T(8,128)(2,1)}) %all-gather.3.cloned.1.call-update) | async-done | bytes 12582928 | tf_op jit(solution)/shard_map/all_gather | solution.py:12
  125.3 6.7 %reduce_sum.30 = bf16[2,768,128]{2,1,0:T(8,128)(2,1)S(1)} reduce(bf16[32,2,768,128]{3,2,1,0:T(8,128)(2,1)} %bitcast.53, bf16[]{:T(256)} %constant.12.clone.1), dimensions={0}, to_apply=%region_0.1 | reduce | flops 6094848 | bytes 12976130 | tf_op jit(solution)/shard_map/reduce_sum | solution.py:12
  132.0 4.8 %fusion.1 = (f32[768]{0:T(1024)S(1)}, f32[3840,768]{1,0:T(8,128)S(1)}) fusion(pred[3840]{0:T(1024)(128)(4,1)S(1)} %concatenate.33, bf16[1536,128]{1,0:T(8,128)(2,1)} %param.6, bf16[3072,128]{1,0:T(8,128)(2,1)} %get-tuple-element.8, bf16[768,128]{1,0:T(8,128)(2,1)S(1)} %get-tuple-element.12), kind=kOutput, calls=%fused_computation.5 | convolution fusion | flops 765787392 | bytes 12983040 | tf_op jit(solution)/shard_map/qhd,khd->hqk/dot_general | solution.py:26
  136.8 0.0 copy-start.3
  136.9 0.0 copy-start.5
  136.9 3.7 %fusion.4 = f32[768]{0:T(1024)S(1)} fusion(f32[3840,768]{1,0:T(8,128)S(1)} %get-tuple-element.18, f32[768]{0:T(1024)S(1)} %get-tuple-element.17, pred[3840]{0:T(1024)(128)(4,1)S(1)} %concatenate.33), kind=kLoop, calls=%fused_computation.8 | loop fusion | flops 14744832 | bytes 11806464 | tf_op jit(solution)/shard_map/reduce_sum | solution.py:32
  140.6 2.3 %fusion = (f32[768]{0:T(1024)S(1)}, f32[4608,768]{1,0:T(8,128)S(1)}) fusion(pred[4608]{0:T(1024)(128)(4,1)S(1)} %concatenate.29, bf16[1536,128]{1,0:T(8,128)(2,1)S(1)} %copy-done.5, bf16[3840,128]{1,0:T(8,128)(2,1)S(1)} %copy-done.3, bf16[768,128]{1,0:T(8,128)(2,1)S(1)} %get-tuple-element.12), kind=kOutput, calls=%fused_computation.2 | convolution fusion | flops 918945024 | bytes 15540224 | tf_op jit(solution)/shard_map/qhd,khd->hqk/dot_general | solution.py:26
  142.9 4.7 %fusion.2 = f32[768]{0:T(1024)S(1)} fusion(f32[4608,768]{1,0:T(8,128)S(1)} %get-tuple-element.20, f32[768]{0:T(1024)S(1)} %get-tuple-element.19, pred[4608]{0:T(1024)(128)(4,1)S(1)} %concatenate.29), kind=kLoop, calls=%fused_computation.6 | loop fusion | flops 17693952 | bytes 14166528 | tf_op jit(solution)/shard_map/reduce_sum | solution.py:32
  147.7 3.1 %fusion.46 = bf16[768,128]{0,1:T(8,128)(2,1)S(1)} fusion(f32[3840,768]{1,0:T(8,128)S(1)} %get-tuple-element.18, f32[768]{0:T(1024)S(1)} %get-tuple-element.17, pred[3840]{0:T(1024)(128)(4,1)S(1)} %concatenate.33, bf16[3072,128]{1,0:T(8,128)(2,1)S(1)} %copy-done.4, bf16[768,128]{1,0:T(8,128)(2,1)S(1)} %get-tuple-element.11, f32[768]{0:T(1024)S(1)} %fusion.4), kind=kOutput, calls=%fused_computation.31 | convolution fusion | flops 771883008 | bytes 12986112 | tf_op jit(solution)/shard_map/hqk,khd->qhd/dot_general | solution.py:34
  150.8 3.7 %fusion.35 = bf16[768,128]{0,1:T(8,128)(2,1)S(1)} fusion(f32[4608,768]{1,0:T(8,128)S(1)} %get-tuple-element.20, f32[768]{0:T(1024)S(1)} %get-tuple-element.19, pred[4608]{0:T(1024)(128)(4,1)S(1)} %concatenate.29, bf16[3840,128]{1,0:T(8,128)(2,1)S(1)} %copy-done.2, bf16[768,128]{1,0:T(8,128)(2,1)S(1)} %get-tuple-element.11, f32[768]{0:T(1024)S(1)} %fusion.2), kind=kOutput, calls=%fused_computation.28 | convolution fusion | flops 926220288 | bytes 15542784 | tf_op jit(solution)/shard_map/hqk,khd->qhd/dot_general | solution.py:34
  154.5 0.9 copy.9
  155.4 12.5 %all_to_all.19 = bf16[8,192,128]{2,1,0:T(8,128)(2,1)S(1)} all-to-all(bf16[8,192,128]{2,1,0:T(8,128)(2,1)} %bitcast.62), channel_id=1, replica_groups=mesh['tm'=32,'head'=8] {'head'}, dimensions={0} | all-to-all | bytes 786432 | tf_op jit(solution)/shard_map/all_to_all | solution.py:66
  167.9 0.0 copy-done
  167.9 1.6 convolution_convert_fusion
  (11 shorter events, 0.1 us)
Async XLA Ops:
  6.5 161.4 %copy-start = (bf16[1024,1536]{1,0:T(8,128)(2,1)S(1)}, bf16[1024,1536]{1,0:T(8,128)(2,1)}, u32[]{:S(2)}) copy-start(bf16[1024,1536]{1,0:T(8,128)(2,1)} %param.11) | copy-start | bytes 9437188
  6.5 26.9 %copy-start.1 = (bf16[1536,128]{1,0:T(8,128)(2,1)S(1)}, bf16[1536,128]{1,0:T(8,128)(2,1)}, u32[]{:S(2)}) copy-start(bf16[1536,128]{1,0:T(8,128)(2,1)} %param.8) | copy-start | bytes 1179652
  6.5 118.7 %all-gather.3.cloned.1.call-start = ((), (), s32[]{:S(2)}) async-start(), calls=%async_computation.1 | async-start | bytes 12976128 | tf_op jit(solution)/shard_map/all_gather | solution.py:12
  11.0 13.2 %collective-permute-start.1 = (bf16[2,1536,128]{2,1,0:T(8,128)(2,1)}, bf16[2,1536,128]{2,1,0:T(8,128)(2,1)}, u32[]{:S(2)}, u32[]{:S(2)}) collective-permute-start(bf16[2,1536,128]{2,1,0:T(8,128)(2,1)} %pad_maximum_fusion), channel_id=1, source_target_pairs={{0,8},{8,16},{16,24},{24,32},{32,40},{40,48},{48,56},{56,64},{64,7... | collective-permute-start | bytes 2359304 | tf_op jit(solution)/shard_map/ppermute | solution.py:18
  13.6 19.8 %collective-permute-start = (bf16[2,768,128]{2,1,0:T(8,128)(2,1)}, bf16[2,768,128]{2,1,0:T(8,128)(2,1)}, u32[]{:S(2)}, u32[]{:S(2)}) collective-permute-start(bf16[2,768,128]{2,1,0:T(8,128)(2,1)} %get-tuple-element.9), channel_id=1, source_target_pairs={{0,16},{8,24},{16,32},{24,40},{32,48},{40,56},{48,64},{56,72},{64,... | collective-permute-start | bytes 1179656 | tf_op jit(solution)/shard_map/ppermute | solution.py:18
  136.8 3.7 %copy-start.3 = (bf16[3840,128]{1,0:T(8,128)(2,1)S(1)}, bf16[3840,128]{1,0:T(8,128)(2,1)}, u32[]{:S(2)}) copy-start(bf16[3840,128]{1,0:T(8,128)(2,1)} %get-tuple-element.6) | copy-start | bytes 2949124
  136.9 3.7 %copy-start.5 = (bf16[1536,128]{1,0:T(8,128)(2,1)S(1)}, bf16[1536,128]{1,0:T(8,128)(2,1)}, u32[]{:S(2)}) copy-start(bf16[1536,128]{1,0:T(8,128)(2,1)} %param.6) | copy-start | bytes 1179652
  142.9 4.7 %copy-start.4 = (bf16[3072,128]{1,0:T(8,128)(2,1)S(1)}, bf16[3072,128]{1,0:T(8,128)(2,1)}, u32[]{:S(2)}) copy-start(bf16[3072,128]{1,0:T(8,128)(2,1)} %get-tuple-element.7) | copy-start | bytes 2359300
  147.6 3.1 %copy-start.2 = (bf16[3840,128]{1,0:T(8,128)(2,1)S(1)}, bf16[3840,128]{1,0:T(8,128)(2,1)}, u32[]{:S(2)}) copy-start(bf16[3840,128]{1,0:T(8,128)(2,1)} %get-tuple-element.5) | copy-start | bytes 2949124
Sparse Core Ops, SparseCore 0:
  9.9 115.3 all-gather.2
